TPU v7x, 32 devices: a whole 2x2x4 slice. The times are simulated.
32 devices in a mesh: dp: 8 (over z, x), lat: 4 (over y, core).
Axes of the slice: x: 2, y: 2, z: 4, core: 2. Of those that a mesh axis runs over, the one named last changes fastest.
Arguments:
- tokens: bfloat16 [24576, 512], P(('dp', 'lat')), may hold values from -6 to 6
- latents: bfloat16 [1536, 1024], P(('dp', 'lat')), may hold values from -6 to 6
- gain_self: float32 [512], replicated, may hold values from 0.1 to 1.9
- w_qkv_tok: bfloat16 [512, 1536], replicated, may hold values from -1 to 1
- w_o_tok: bfloat16 [512, 512], replicated, may hold values from -0.25 to 0.25
- gain_read: float32 [512], replicated, may hold values from 0.1 to 1.9
- w_kv_read: bfloat16 [512, 2048], replicated, may hold values from -1 to 1
- gain_lat: float32 [1024], replicated, may hold values from 0.1 to 1.9
- w_q_read: bfloat16 [1024, 1024], replicated, may hold values from -1 to 1
- gain_glob: float32 [1024], replicated, may hold values from 0.1 to 1.9
- w_qkv_glob: bfloat16 [3, 1024, 1024], P(None, None, 'lat'), may hold values from -1 to 1
- w_o_glob: bfloat16 [1024, 1024], P('lat'), may hold values from -0.375 to 0.375
- gain_write: float32 [512], replicated, may hold values from 0.1 to 1.9
- w_q_write: bfloat16 [512, 512], replicated, may hold values from -1 to 1
- gain_wlat: float32 [1024], replicated, may hold values from 0.1 to 1.9
- w_kv_write: bfloat16 [1024, 1024], replicated, may hold values from -1 to 1
Outputs:
- tokens_out: bfloat16 [24576, 512], P(('dp', 'lat'))
- latents_out: bfloat16 [1536, 1024], P(('dp', 'lat'))
All inputs are finite; a program needn't handle non-finite values.
Results may differ from a plain program's by a relative error of at most 0.015.
Values may be sent and summed in bfloat16 or wider, within the bound.
A program may use at most 128 MiB of HBM per device.

v0:
```python
import jax
import jax.numpy as jnp
from jax import lax
from jax.sharding import PartitionSpec as P

HEAD = 64
G = 256
NLAT = 16


def rms_norm(values, gain):
    floats = values.astype(jnp.float32)
    factor = lax.rsqrt(jnp.mean(floats * floats, axis=-1, keepdims=True) + 1e-06)
    return (floats * factor * gain).astype(jnp.bfloat16)


def attend(query, keys, values):
    scores = jnp.einsum("qhe,khe->hqk", query, keys, preferred_element_type=jnp.float32) * HEAD ** (
        -0.5
    )
    peak = jnp.max(scores, axis=-1, keepdims=True)
    weights = jnp.exp(scores - peak)
    total = jnp.sum(weights, axis=-1)
    mixed = jnp.einsum(
        "hqk,khe->hqe", weights.astype(jnp.bfloat16), values, preferred_element_type=jnp.float32
    )
    return jnp.transpose(mixed / total[:, :, None], (1, 0, 2))


def front(group, lat_rows, gain_self, w_qkv_tok, w_o_tok, gain_read, w_kv_read, gain_lat, w_q_read):
    rows = group.shape[0]
    packed = jnp.dot(rms_norm(group, gain_self), w_qkv_tok, preferred_element_type=jnp.float32)
    packed = packed.astype(jnp.bfloat16).reshape(rows, 3, -1, HEAD)
    mixed = attend(packed[:, 0], packed[:, 1], packed[:, 2]).reshape(rows, -1).astype(jnp.bfloat16)
    tokens_mid = (
        group.astype(jnp.float32) + jnp.dot(mixed, w_o_tok, preferred_element_type=jnp.float32)
    ).astype(jnp.bfloat16)
    key_vals = jnp.dot(
        rms_norm(tokens_mid, gain_read), w_kv_read, preferred_element_type=jnp.float32
    )
    key_vals = key_vals.astype(jnp.bfloat16).reshape(rows, 2, -1, HEAD)
    query = jnp.dot(rms_norm(lat_rows, gain_lat), w_q_read, preferred_element_type=jnp.float32)
    query = query.astype(jnp.bfloat16).reshape(lat_rows.shape[0], -1, HEAD)
    read = attend(query, key_vals[:, 0], key_vals[:, 1]).reshape(lat_rows.shape[0], -1)
    return (tokens_mid, (lat_rows.astype(jnp.float32) + read).astype(jnp.bfloat16))


def back(tokens_mid, lat_rows, gain_write, w_q_write, gain_wlat, w_kv_write):
    rows = tokens_mid.shape[0]
    query = jnp.dot(rms_norm(tokens_mid, gain_write), w_q_write, preferred_element_type=jnp.float32)
    query = query.astype(jnp.bfloat16).reshape(rows, -1, HEAD)
    key_vals = jnp.dot(
        rms_norm(lat_rows, gain_wlat), w_kv_write, preferred_element_type=jnp.float32
    )
    key_vals = key_vals.astype(jnp.bfloat16).reshape(lat_rows.shape[0], 2, -1, HEAD)
    written = attend(query, key_vals[:, 0], key_vals[:, 1]).reshape(rows, -1)
    return (tokens_mid.astype(jnp.float32) + written).astype(jnp.bfloat16)


def local(
    tokens,
    latents,
    gain_self,
    w_qkv_tok,
    w_o_tok,
    gain_read,
    w_kv_read,
    gain_lat,
    w_q_read,
    gain_glob,
    w_qkv_glob,
    w_o_glob,
    gain_write,
    w_q_write,
    gain_wlat,
    w_kv_write,
):
    width = tokens.shape[1]
    lat_width = latents.shape[1]
    groups = tokens.reshape(-1, G, width)
    lat_groups = latents.reshape(-1, NLAT, lat_width)
    tokens_mid, latents_mid = jax.vmap(
        lambda group, lat_rows: front(
            group, lat_rows, gain_self, w_qkv_tok, w_o_tok, gain_read, w_kv_read, gain_lat, w_q_read
        )
    )(groups, lat_groups)
    latents_mid = latents_mid.reshape(-1, lat_width)
    normed = rms_norm(latents_mid, gain_glob)
    block = lax.all_gather(normed, "lat", axis=0, tiled=True)
    block_rows = block.shape[0]
    heads_here = w_qkv_glob.shape[2] // HEAD
    dp_count = lax.axis_size("dp")
    blocks = dp_count // heads_here
    part_rows = block_rows // blocks

    def head_major(which):
        weight = w_qkv_glob[which].reshape(lat_width, heads_here, HEAD)
        return jnp.einsum("rd,dhe->hre", block, weight, preferred_element_type=jnp.float32).astype(
            jnp.bfloat16
        )

    def fan_out(projected):
        spread = projected.reshape(heads_here, 1, block_rows * HEAD)
        return jnp.broadcast_to(spread, (heads_here, blocks, block_rows * HEAD)).reshape(
            dp_count, block_rows * HEAD
        )

    key_rows, value_rows = (
        lax.all_to_all(fan_out(head_major(1)), "dp", split_axis=0, concat_axis=0, tiled=True),
        lax.all_to_all(fan_out(head_major(2)), "dp", split_axis=0, concat_axis=0, tiled=True),
    )
    all_keys = key_rows.reshape(-1, 1, HEAD)
    all_values = value_rows.reshape(-1, 1, HEAD)
    query_send = head_major(0).reshape(dp_count, part_rows, HEAD)
    received = lax.all_to_all(query_send, "dp", split_axis=0, concat_axis=0, tiled=True)
    item_count = received.shape[1]
    query_rows = received.reshape(dp_count * item_count, 1, HEAD)
    mixed_rows = attend(query_rows, all_keys, all_values).astype(jnp.bfloat16)
    returned = lax.all_to_all(
        mixed_rows.reshape(dp_count, item_count, HEAD),
        "dp",
        split_axis=0,
        concat_axis=0,
        tiled=True,
    )
    mixed = jnp.transpose(returned.reshape(heads_here, block_rows, HEAD), (1, 0, 2)).reshape(
        block_rows, heads_here * HEAD
    )
    summed = lax.psum_scatter(
        jnp.dot(mixed, w_o_glob, preferred_element_type=jnp.float32).astype(jnp.bfloat16),
        "lat",
        scatter_dimension=0,
        tiled=True,
    ).astype(jnp.float32)
    latents_out = (latents_mid.astype(jnp.float32) + summed).astype(jnp.bfloat16)
    tokens_out = jax.vmap(
        lambda tok_rows, lat_rows: back(
            tok_rows, lat_rows, gain_write, w_q_write, gain_wlat, w_kv_write
        )
    )(tokens_mid, latents_out.reshape(-1, NLAT, lat_width))
    return (tokens_out.reshape(-1, width), latents_out)


def solution(mesh):
    placed = (
        P(("dp", "lat"), None),
        P(("dp", "lat"), None),
        P(),
        P(),
        P(),
        P(),
        P(),
        P(),
        P(),
        P(),
        P(None, None, "lat"),
        P("lat", None),
        P(),
        P(),
        P(),
        P(),
    )
    return jax.shard_map(
        local,
        mesh=mesh,
        in_specs=placed,
        out_specs=(P(("dp", "lat"), None), P(("dp", "lat"), None)),
        check_vma=False,
    )
```

profile of v0, /device:TPU:0, one launch (start us, length us, event | category | flops | bytes accessed | tf_op | source)
XLA Modules:
  0.0 139.4 jit_solution(9101611196425084850)
XLA Ops:
  7.2 1.5 %multiply_reduce_fusion.2 = f32[768]{0:T(1024)S(1)} fusion(bf16[768,512]{1,0:T(8,128)(2,1)} %param.16), kind=kLoop, calls=%fused_computation.38 | loop fusion | flops 1178880 | bytes 789504 | tf_op jit(solution)/shard_map/vmap()/reduce_sum | solution.py:13
  8.7 4.5 %convolution_convert_fusion.1 = bf16[3,256,1536]{2,1,0:T(8,128)(2,1)} fusion(bf16[512,1536]{1,0:T(8,128)(2,1)} %param.19, f32[512]{0:T(512)} %param.18, f32[3,256]{1,0:T(4,128)S(1)} %rsqrt.51, bf16[3,256,512]{2,1,0:T(8,128)(2,1)} %bitcast.153), kind=kOutput, calls=%fused_computation.9 | convolution fusion | flops 1210712064 | bytes 4723712 | tf_op jit(solution)/shard_map/vmap()/dot_general | solution.py:32
  13.2 4.3 %copy.101 = bf16[3,256,1536]{1,2,0:T(8,128)(2,1)} copy(bf16[3,256,1536]{2,1,0:T(8,128)(2,1)} %convolution_convert_fusion.1) | data formatting | bytes 4718592 | tf_op jit(solution)/shard_map/vmap()/convert_element_type | solution.py:33
  17.5 2.4 %multiply_reduce_fusion = (f32[3,8,256]{2,1,0:T(8,128)S(1)}, f32[3,8,256,256]{2,3,1,0:T(8,128)S(1)}) fusion(bf16[3,256,3,8,64]{1,4,3,2,0:T(8,128)(2,1)} %bitcast.145), kind=kOutput, calls=%fused_computation.1 | convolution fusion | flops 204466176 | bytes 7888896 | tf_op jit(solution)/shard_map/vmap(qhe,khe->hqk)/dot_general | solution.py:18
  21.0 2.5 %fusion.23 = bf16[3,256,8,64]{1,3,2,0:T(8,128)(2,1)S(1)} fusion(f32[3,8,256,256]{2,3,1,0:T(8,128)S(1)} %get-tuple-element.9, f32[3,8,256]{2,1,0:T(8,128)S(1)} %get-tuple-element.8, bf16[3,256,3,8,64]{1,4,3,2,0:T(8,128)(2,1)} %bitcast.146, f32[3,256,8]{1,2,0:T(8,128)S(1)} %bitcast.159), kind=kOutput, calls=%fused_computation.34 | convolution fusion | flops 206831616 | bytes 7913472 | tf_op jit(solution)/shard_map/vmap(hqk,khe->hqe)/dot_general | solution.py:24
  25.2 3.5 %convolution_convert_fusion = bf16[3,256,2048]{2,1,0:T(8,128)(2,1)} fusion(bf16[512,2048]{1,0:T(8,128)(2,1)S(1)} %copy-done, bf16[3,256,512]{2,1,0:T(8,128)(2,1)S(1)} %get-tuple-element.11, f32[512]{0:T(512)S(1)} %copy-done.12, f32[3,256]{1,0:T(4,128)S(1)} %add_rsqrt_fusion), kind=kOutput, calls=%fused_computation.8 | convolution fusion | flops 1613758464 | bytes 6034432 | tf_op jit(solution)/shard_map/vmap()/dot_general | solution.py:38
  28.7 4.7 %copy.108 = bf16[3,256,2048]{1,2,0:T(8,128)(2,1)} copy(bf16[3,256,2048]{2,1,0:T(8,128)(2,1)} %convolution_convert_fusion) | data formatting | bytes 6291456 | tf_op jit(solution)/shard_map/vmap()/convert_element_type | solution.py:41
  33.6 2.1 %fusion.36 = bf16[3,16,1024]{2,1,0:T(8,128)(2,1)S(1)} fusion(bf16[1024,1024]{1,0:T(8,128)(2,1)} %param.24, f32[1024]{0:T(1024)S(1)} %copy-done.8, f32[3,16]{1,0:T(4,128)S(1)} %rsqrt.54, bf16[3,16,1024]{2,1,0:T(8,128)(2,1)S(1)} %bitcast.152), kind=kOutput, calls=%fused_computation.47 | convolution fusion | flops 100909056 | bytes 2298048 | tf_op jit(solution)/shard_map/vmap()/dot_general | solution.py:42
  35.9 2.0 %fusion.83 = (f32[3,16,16]{2,1,0:T(8,128)S(1)}, f32[3,16,16,256]{3,2,1,0:T(8,128)S(1)}) fusion(bf16[3,256,2,16,64]{1,4,3,2,0:T(8,128)(2,1)} %bitcast.143, bf16[3,16,16,64]{3,2,1,0:T(8,128)(2,1)S(1)} %reshape.186), kind=kOutput, calls=%fused_computation.108 | convolution fusion | flops 25558272 | bytes 2460672 | tf_op jit(solution)/shard_map/vmap(qhe,khe->hqk)/dot_general | solution.py:18
  39.4 8.0 %all_gather.3 = bf16[192,1024]{1,0:T(8,128)(2,1)S(1)} all-gather(bf16[48,1024]{1,0:T(8,128)(2,1)S(1)} %fusion.70), channel_id=1, replica_groups=mesh['dp'=8,'lat'=4] {'lat'}, dimensions={0}, use_global_device_ids=true | all-gather | bytes 491520 | tf_op jit(solution)/shard_map/all_gather | solution.py:89
  47.4 1.4 fusion.57
  49.7 5.8 %all-to-all-start = ((bf16[8,96,64]{1,2,0:T(8,128)(2,1)}), bf16[8,96,64]{1,2,0:T(8,128)(2,1)S(1)}, u32[]{:S(2)}, u32[]{:S(2)}) async-start(bf16[8,96,64]{1,2,0:T(8,128)(2,1)} %copy.115), calls=%async_computation | async-start | bytes 262144 | tf_op jit(solution)/shard_map/all_to_all | solution.py:115
  55.5 1.4 fusion.55
  58.1 1.8 %reduce.10 = bf16[8,12288]{1,0:T(8,128)(2,1)S(1)} reduce(bf16[8,1,12288]{2,1,0:T(2,128)(2,1)S(1)} %all_to_all.24, bf16[]{:T(256)} %broadcast.118), dimensions={1}, to_apply=%all_to_all.24.reduce_sub_computation | reduce | bytes 393218 | tf_op jit(solution)/shard_map/all_to_all | solution.py:109
  60.7 2.3 %all-to-all-done = bf16[8,96,64]{1,2,0:T(8,128)(2,1)S(1)} async-done(((bf16[8,96,64]{1,2,0:T(8,128)(2,1)}), bf16[8,96,64]{1,2,0:T(8,128)(2,1)S(1)}, u32[]{:S(2)}, u32[]{:S(2)}) %all-to-all-start) | async-done | bytes 98336 | tf_op jit(solution)/shard_map/all_to_all | solution.py:115
  63.0 3.7 %all-to-all-start.1 = ((bf16[8,2,6144]{2,1,0:T(2,128)(2,1)}), bf16[8,2,6144]{2,1,0:T(2,128)(2,1)S(1)}, u32[]{:S(2)}, u32[]{:S(2)}) async-start(bf16[8,2,6144]{2,1,0:T(2,128)(2,1)} %reshape.217), calls=%async_computation.1 | async-start | bytes 393216 | tf_op jit(solution)/shard_map/all_to_all | solution.py:109
  66.7 1.4 fusion.53
  68.8 1.8 %reduce.9 = bf16[8,12288]{1,0:T(8,128)(2,1)S(1)} reduce(bf16[8,1,12288]{2,1,0:T(2,128)(2,1)S(1)} %all_to_all.25, bf16[]{:T(256)} %broadcast.118), dimensions={1}, to_apply=%all_to_all.25.reduce_sub_computation | reduce | bytes 393218 | tf_op jit(solution)/shard_map/all_to_all | solution.py:110
  71.4 3.2 %all-to-all-done.1 = bf16[8,2,6144]{2,1,0:T(2,128)(2,1)S(1)} async-done(((bf16[8,2,6144]{2,1,0:T(2,128)(2,1)}), bf16[8,2,6144]{2,1,0:T(2,128)(2,1)S(1)}, u32[]{:S(2)}, u32[]{:S(2)}) %all-to-all-start.1) | async-done | bytes 196640 | tf_op jit(solution)/shard_map/all_to_all | solution.py:109
  74.6 3.4 %all-to-all-start.2 = ((bf16[8,2,6144]{2,1,0:T(2,128)(2,1)}), bf16[8,2,6144]{2,1,0:T(2,128)(2,1)S(1)}, u32[]{:S(2)}, u32[]{:S(2)}) async-start(bf16[8,2,6144]{2,1,0:T(2,128)(2,1)} %reshape.215), calls=%async_computation.2 | async-start | bytes 393216 | tf_op jit(solution)/shard_map/all_to_all | solution.py:110
  78.5 1.2 reduce.7
  80.1 5.7 %all-to-all-done.2 = bf16[8,2,6144]{2,1,0:T(2,128)(2,1)S(1)} async-done(((bf16[8,2,6144]{2,1,0:T(2,128)(2,1)}), bf16[8,2,6144]{2,1,0:T(2,128)(2,1)S(1)}, u32[]{:S(2)}, u32[]{:S(2)}) %all-to-all-start.2) | async-done | bytes 196640 | tf_op jit(solution)/shard_map/all_to_all | solution.py:110
  86.0 1.2 reduce.8
  90.5 10.2 %all_to_all.30 = bf16[8,96,64]{1,2,0:T(8,128)(2,1)S(1)} all-to-all(bf16[8,96,64]{1,2,0:T(8,128)(2,1)S(1)} %copy.123), channel_id=1, replica_groups=mesh['dp'=8,'lat'=4] {'dp'}, dimensions={0} | all-to-all | bytes 196608 | tf_op jit(solution)/shard_map/all_to_all | solution.py:119
  101.0 2.1 %convolution_convert_fusion.3 = bf16[192,1024]{1,0:T(8,128)(2,1)} fusion(bf16[192,256]{0,1:T(8,128)(2,1)S(1)} %bitcast.157, bf16[256,1024]{1,0:T(8,128)(2,1)} %param.27), kind=kOutput, calls=%fused_computation.41 | convolution fusion | flops 100859904 | bytes 1015808 | tf_op jit(solution)/shard_map/dot_general | solution.py:130
  103.1 2.6 %convolution_convert_fusion.2 = bf16[3,256,512]{2,1,0:T(8,128)(2,1)} fusion(bf16[3,256,512]{2,1,0:T(8,128)(2,1)S(1)} %copy-done.5, f32[512]{0:T(512)S(1)} %copy-done.13, f32[3,256]{1,0:T(4,128)S(1)} %add_rsqrt_fusion, bf16[512,512]{1,0:T(8,128)(2,1)} %param.29), kind=kOutput, calls=%fused_computation.39 | convolution fusion | flops 404619264 | bytes 2102272 | tf_op jit(solution)/shard_map/vmap()/dot_general | solution.py:50
  105.7 1.4 %copy.107 = bf16[3,256,512]{1,2,0:T(8,128)(2,1)S(1)} copy(bf16[3,256,512]{2,1,0:T(8,128)(2,1)} %convolution_convert_fusion.2) | data formatting | bytes 1572864 | tf_op jit(solution)/shard_map/vmap()/convert_element_type | solution.py:51
  107.1 14.4 %reduce-scatter.2.cloned.1.call-done = bf16[48,1024]{1,0:T(8,128)(2,1)} async-done(((bf16[192,1024]{1,0:T(8,128)(2,1)}), bf16[48,1024]{1,0:T(8,128)(2,1)}) %reduce-scatter.2.cloned.1.call-update) | async-done | bytes 98320 | tf_op jit(solution)/shard_map/reduce_scatter | solution.py:129
  122.6 2.1 %fusion.39 = bf16[3,16,1024]{2,1,0:T(8,128)(2,1)S(1)} fusion(bf16[1024,1024]{1,0:T(8,128)(2,1)} %param.31, f32[1024]{0:T(1024)S(1)} %copy-done.9, f32[3,16]{1,0:T(4,128)S(1)} %rsqrt.57, bf16[3,16,1024]{2,1,0:T(8,128)(2,1)S(1)} %bitcast.158), kind=kOutput, calls=%fused_computation.48 | convolution fusion | flops 100909056 | bytes 2298048 | tf_op jit(solution)/shard_map/vmap()/dot_general | solution.py:52
  125.3 1.6 %bitcast_divide_fusion = f32[3,256,8,64]{1,3,2,0:T(8,128)} fusion(f32[3,256,8]{1,2,0:T(8,128)S(1)} %bitcast.161, f32[3,8,256,16]{2,3,1,0:T(8,128)S(1)} %get-tuple-element.17, f32[3,8,256]{2,1,0:T(8,128)S(1)} %get-tuple-element.16, bf16[3,16,1,8,64]{4,3,2,1,0:T(8,128)(2,1)S(1)} %get-tuple-element.6), kind=kOutput, calls=%fused_computation.32 | convolution fusion | flops 13172736 | bytes 2064384 | tf_op jit(solution)/shard_map/vmap(hqk,khe->hqe)/dot_general | solution.py:24
  126.9 3.1 %copy.128 = f32[3,256,512]{2,1,0:T(8,128)} copy(f32[3,256,512]{1,2,0:T(8,128)} %bitcast.148) | data formatting | bytes 3145728 | tf_op jit(solution)/shard_map/vmap()/reshape | solution.py:56
  130.0 2.5 %fusion.20 = bf16[3,256,512]{2,1,0:T(8,128)(2,1)} fusion(f32[3,256,512]{2,1,0:T(8,128)} %copy.128, bf16[3,256,512]{2,1,0:T(8,128)(2,1)S(1)} %copy-done.6), kind=kLoop, calls=%fused_computation.27 | loop fusion | flops 1179648 | bytes 3145728 | tf_op jit(solution)/shard_map/vmap()/convert_element_type | solution.py:57
  (84 shorter events, 15.2 us)
Async XLA Ops:
  7.2 18.0 %copy-start = (bf16[512,2048]{1,0:T(8,128)(2,1)S(1)}, bf16[512,2048]{1,0:T(8,128)(2,1)}, u32[]{:S(2)}) copy-start(bf16[512,2048]{1,0:T(8,128)(2,1)} %param.22) | copy-start | bytes 6291460
  21.0 2.5 %copy-start.3 = (bf16[768,512]{1,0:T(8,128)(2,1)S(1)}, bf16[768,512]{1,0:T(8,128)(2,1)}, u32[]{:S(2)}) copy-start(bf16[768,512]{1,0:T(8,128)(2,1)} %param.16) | copy-start | bytes 2359300
  21.0 2.5 %copy-start.11 = (bf16[512,512]{1,0:T(8,128)(2,1)S(1)}, bf16[512,512]{1,0:T(8,128)(2,1)}, u32[]{:S(2)}) copy-start(bf16[512,512]{1,0:T(8,128)(2,1)} %param.20) | copy-start | bytes 1572868
  23.5 1.6 %copy-start.12 = (f32[512]{0:T(512)S(1)}, f32[512]{0:T(512)}, u32[]{:S(2)}) copy-start(f32[512]{0:T(512)} %param.21) | copy-start | bytes 6148
  24.3 0.9 copy-start.4
  28.7 4.7 %copy-start.2 = (bf16[48,1024]{1,0:T(8,128)(2,1)S(1)}, bf16[48,1024]{1,0:T(8,128)(2,1)}, u32[]{:S(2)}) copy-start(bf16[48,1024]{1,0:T(8,128)(2,1)} %param.17) | copy-start | bytes 294916
  28.7 5.0 %copy-start.8 = (f32[1024]{0:T(1024)S(1)}, f32[1024]{0:T(1024)}, u32[]{:S(2)}) copy-start(f32[1024]{0:T(1024)} %param.23) | copy-start | bytes 12292
  35.9 2.4 %copy-start.1 = (bf16[3,256,2048]{1,2,0:T(8,128)(2,1)S(1)}, bf16[3,256,2048]{1,2,0:T(8,128)(2,1)}, u32[]{:S(2)}) copy-start(bf16[3,256,2048]{1,2,0:T(8,128)(2,1)} %copy.108) | copy-start | bytes 9437188
  38.3 1.0 copy-start.10
  49.7 13.3 %all-to-all-start = ((bf16[8,96,64]{1,2,0:T(8,128)(2,1)}), bf16[8,96,64]{1,2,0:T(8,128)(2,1)S(1)}, u32[]{:S(2)}, u32[]{:S(2)}) async-start(bf16[8,96,64]{1,2,0:T(8,128)(2,1)} %copy.115), calls=%async_computation | async-start | bytes 262144 | tf_op jit(solution)/shard_map/all_to_all | solution.py:115
  63.0 11.6 %all-to-all-start.1 = ((bf16[8,2,6144]{2,1,0:T(2,128)(2,1)}), bf16[8,2,6144]{2,1,0:T(2,128)(2,1)S(1)}, u32[]{:S(2)}, u32[]{:S(2)}) async-start(bf16[8,2,6144]{2,1,0:T(2,128)(2,1)} %reshape.217), calls=%async_computation.1 | async-start | bytes 393216 | tf_op jit(solution)/shard_map/all_to_all | solution.py:109
  74.6 11.1 %all-to-all-start.2 = ((bf16[8,2,6144]{2,1,0:T(2,128)(2,1)}), bf16[8,2,6144]{2,1,0:T(2,128)(2,1)S(1)}, u32[]{:S(2)}, u32[]{:S(2)}) async-start(bf16[8,2,6144]{2,1,0:T(2,128)(2,1)} %reshape.215), calls=%async_computation.2 | async-start | bytes 393216 | tf_op jit(solution)/shard_map/all_to_all | solution.py:110
  78.0 43.4 %reduce-scatter.2.cloned.1.call-start = ((), (), s32[]{:S(2)}) async-start(), calls=%async_computation.5 | async-start | bytes 491520 | tf_op jit(solution)/shard_map/reduce_scatter | solution.py:129
  90.3 12.8 %copy-start.5 = (bf16[3,256,512]{2,1,0:T(8,128)(2,1)S(1)}, bf16[3,256,512]{2,1,0:T(8,128)(2,1)}, u32[]{:S(2)}) copy-start(bf16[3,256,512]{2,1,0:T(8,128)(2,1)} %copy-done.4) | copy-start | bytes 2359300
  90.3 12.7 %copy-start.13 = (f32[512]{0:T(512)S(1)}, f32[512]{0:T(512)}, u32[]{:S(2)}) copy-start(f32[512]{0:T(512)} %param.28) | copy-start | bytes 6148
  103.1 19.5 %copy-start.9 = (f32[1024]{0:T(1024)S(1)}, f32[1024]{0:T(1024)}, u32[]{:S(2)}) copy-start(f32[1024]{0:T(1024)} %param.30) | copy-start | bytes 12292
  122.5 2.7 %copy-start.7 = (bf16[48,1024]{1,0:T(8,128)(2,1)}, bf16[48,1024]{1,0:T(8,128)(2,1)S(1)}, u32[]{:S(2)}) copy-start(bf16[48,1024]{1,0:T(8,128)(2,1)S(1)} %get-tuple-element.3) | copy-start | bytes 294916
  126.9 3.1 %copy-start.6 = (bf16[3,256,512]{2,1,0:T(8,128)(2,1)S(1)}, bf16[3,256,512]{2,1,0:T(8,128)(2,1)}, u32[]{:S(2)}) copy-start(bf16[3,256,512]{2,1,0:T(8,128)(2,1)} %copy-done.4) | copy-start | bytes 2359300
Sparse Core Ops, SparseCore 0:
  103.2 18.2 reduce-scatter.1
where the time goes:
time: 141 us; the launch traced here: 139 us
  matrix products  33 us (23%)
  waiting for transfers between devices  25.7 us (18%)
  local copies, waits for them, and re-layouts  21.4 us (15%)
  blocking collectives  18.1 us (13%)
  between operations  14.5 us (10%)
  other arithmetic  13.8 us (10%)
  starting transfers between devices  12.9 us (9%)
    reduce_scatter x1, waiting for transfers between devices, local(): lax.psum_scatter(jnp.dot(mixed, w_o_glob, preferred_element_type=jnp.floa...  14.4 us
    all_to_all x1, blocking collectives, local(): lax.all_to_all(mixed_rows.reshape(dp_count, item_count, HEAD), 'dp', spli...  10.2 us
    all_gather x1, blocking collectives, local(): block = lax.all_gather(normed, 'lat', axis=0, tiled=True)  7.97 us
    all_to_all x1, starting transfers between devices, local(): lax.all_to_all(query_send, 'dp', split_axis=0, concat_axis=0, tiled=True)  5.82 us
    all_to_all x1, waiting for transfers between devices, local(): lax.all_to_all(fan_out(head_major(2)), 'dp', split_axis=0, concat_axis=0,...  5.71 us
    dot_general x4, matrix products, attend(): jnp.einsum('hqk,khe->hqe', weights.astype(jnp.bfloat16), values, preferre...  5.68 us
    dot_general x4, matrix products, attend(): jnp.einsum('qhe,khe->hqk', query, keys, preferred_element_type=jnp.float32)  5.49 us
    convert_element_type x1, local copies, waits for them, and re-layouts, front(): key_vals = key_vals.astype(jnp.bfloat16).reshape(rows, 2, -1, HEAD)  4.73 us
  transfers between devices with their start and end apart: 4, of which 4 were waited for; matrix products, arithmetic and copies ran while one was open for 11% of the time, Pallas kernels for 0%

commit v1 on v0

v1 whole, which is shorter than its diff:
```python
import functools

import jax
import jax.numpy as jnp
from jax import lax
from jax.experimental import pallas as pl
from jax.experimental.pallas import tpu as pltpu
from jax.sharding import PartitionSpec as P

HEAD = 64
G = 256
NLAT = 16
SCALE = HEAD ** (-0.5)
MESH = pl.DeviceIdType.MESH
F32 = jnp.float32
BF16 = jnp.bfloat16


def rms_norm(values, gain):
    floats = values.astype(F32)
    factor = lax.rsqrt(jnp.mean(floats * floats, axis=-1, keepdims=True) + 1e-06)
    return (floats * factor * gain).astype(BF16)


def dot(a, b):
    return jnp.dot(a, b, preferred_element_type=F32)


def dot_nt(a, b):
    return lax.dot_general(a, b, (((1,), (1,)), ((), ())), preferred_element_type=F32)


def dot_tn(a, b):
    return lax.dot_general(a, b, (((0,), (0,)), ((), ())), preferred_element_type=F32)


def spread_heads(query, count):
    lane_head = lax.broadcasted_iota(jnp.int32, query.shape, 1) // HEAD
    zero = jnp.zeros_like(query)
    return jnp.concatenate([jnp.where(lane_head == h, query, zero) for h in range(count)], axis=0)


def fold_heads(stacked, count):
    rows = stacked.shape[0] // count
    lane_head = lax.broadcasted_iota(jnp.int32, (rows, stacked.shape[1]), 1) // HEAD
    out = stacked[:rows]
    for h in range(1, count):
        out = jnp.where(lane_head == h, stacked[h * rows : (h + 1) * rows], out)
    return out


def softmax_mix(stacked, keys, values):
    scores = dot_nt(stacked, keys)
    peak = jnp.max(scores, axis=-1, keepdims=True)
    weights = jnp.exp(scores - peak)
    total = jnp.sum(weights, axis=-1, keepdims=True)
    return dot(weights.astype(BF16), values) * (1.0 / total)


def kernel(
    dp_count,
    lat_count,
    tok,
    lat_in,
    g_self,
    w_qkv_h,
    w_o_h,
    g_read,
    w_kvr_h,
    g_lat,
    w_qr_h,
    g_glob,
    w_glob_h,
    w_og_h,
    g_write,
    w_qw_h,
    g_wlat,
    w_kvw_h,
    tok_out,
    lat_out,
    w_qkv,
    w_o,
    w_kvr,
    w_qr,
    w_glob,
    w_og,
    w_qw,
    w_kvw,
    mid,
    lmid,
    rq,
    packed,
    mixed,
    kvr,
    gath,
    kv,
    qq,
    msend,
    mrecv,
    lfin,
    load_sem,
    z_send,
    z_recv,
    p_send,
    p_recv,
    c_send,
    c_recv,
    wo_send,
    wo_recv,
    m_send,
    m_recv,
):
    width = tok.shape[1]
    lat_width = lat_in.shape[1]
    groups = tok.shape[0] // G
    lat_rows = lat_in.shape[0]
    nz = dp_count // 2
    dp = lax.axis_index("dp")
    lat = lax.axis_index("lat")
    z, x = dp // 2, dp % 2
    y, core = lat // 2, lat % 2
    dp_x = dp + 1 - 2 * x
    lat_y = (lat + 2) % 4
    partner = lat + 1 - 2 * core
    diag = (partner + 2) % 4
    a = (1 - core) * y + core * x
    b = (1 - core) * x + core * y
    first = ((1 - core) * dp + core * dp_x, (1 - core) * lat_y + core * lat)
    second = ((1 - core) * dp_x + core * dp, (1 - core) * lat + core * lat_y)
    base = (b * 2 + a) * nz
    other = (b * 2 + 1 - a) * nz
    me = base + z

    loads = []
    for i, (src, dst) in enumerate(
        ((w_qkv_h, w_qkv), (w_o_h, w_o), (w_qr_h, w_qr), (w_kvr_h, w_kvr), (w_glob_h, w_glob),
         (w_qw_h, w_qw), (w_kvw_h, w_kvw), (w_og_h, w_og.at[lat]))
    ):
        loads.append(pltpu.make_async_copy(src, dst, load_sem.at[i]))
        loads[-1].start()

    barrier = pltpu.get_barrier_semaphore()

    def greet(offset, carry):
        pl.semaphore_signal(
            barrier, inc=1, device_id=((z + offset) % nz * 2 + x, lat), device_id_type=MESH
        )
        return carry

    lax.fori_loop(1, nz, greet, 0)
    for peer in ((dp_x, lat), (dp, lat_y), (dp, partner), (dp, diag)):
        pl.semaphore_signal(barrier, inc=1, device_id=peer, device_id_type=MESH)
    pl.semaphore_wait(barrier, nz + 3)

    def remote(src, dst, send_sem, recv_sem, peer):
        return pltpu.make_async_remote_copy(
            src_ref=src, dst_ref=dst, send_sem=send_sem, recv_sem=recv_sem, device_id=peer,
            device_id_type=MESH,
        )

    wo_first = [
        remote(w_og_h, w_og.at[lat], wo_send.at[0], wo_recv.at[0], (dp, partner)),
        remote(w_og_h, w_og.at[lat], wo_send.at[1], wo_recv.at[1], (dp, lat_y)),
    ]
    wo_relay = remote(w_og.at[lat_y], w_og.at[lat_y], wo_send.at[2], wo_recv.at[2], (dp, partner))
    for copy in wo_first:
        copy.start()

    def piece(g, start, count):
        return gath.at[g, core, pl.ds(start, count)]

    def along(ref, send_sem, recv_sem, peer):
        return remote(ref, ref, send_sem, recv_sem, peer)

    to_first = [along(piece(g, base, nz), p_send.at[g, 0], p_recv.at[g, 0], first) for g in range(groups)]
    to_second = [
        along(piece(g, b * 2 * nz, 2 * nz), p_send.at[g, 1], p_recv.at[g, 1], second)
        for g in range(groups)
    ]
    shares = [
        [
            along(piece(g, start, count), c_send.at[g, i], c_recv.at[g, i], (dp, partner))
            for i, (start, count) in enumerate(
                ((base, nz), (other, nz), ((1 - b) * 2 * nz, 2 * nz))
            )
        ]
        for g in range(groups)
    ]

    def z_start(g):
        def one(offset, carry):
            remote(
                gath.at[g, core, me], gath.at[g, core, me], z_send.at[g], z_recv.at[g],
                ((z + offset) % nz * 2 + x, lat),
            ).start()
            return carry

        lax.fori_loop(1, nz, one, 0)

    def z_wait(g, sem):
        ref = piece(g, base, nz - 1)
        pltpu.make_async_copy(ref, ref, sem.at[g]).wait()

    def stage_one(g):
        z_wait(g, z_recv)
        to_first[g].start()
        shares[g][0].start()

    def stage_two(g):
        to_first[g].wait_recv()
        to_second[g].start()
        shares[g][1].start()

    def stage_three(g):
        to_second[g].wait_recv()
        shares[g][2].start()

    def self_part(g):
        rows = pl.ds(g * G, G)
        group = tok[rows, :]
        normed = rms_norm(group, g_self[...])
        if g == 0:
            loads[0].wait()
        packed[...] = dot(normed, w_qkv[...]).astype(BF16)
        for pair in range(width // (2 * HEAD)):
            at = pair * 2 * HEAD
            query = packed[:, at : at + 2 * HEAD] * jnp.asarray(SCALE, BF16)
            keys = packed[:, width + at : width + at + 2 * HEAD]
            values = packed[:, 2 * width + at : 2 * width + at + 2 * HEAD]
            out = softmax_mix(spread_heads(query, 2), keys, values)
            mixed[:, at : at + 2 * HEAD] = fold_heads(out, 2).astype(BF16)
        if g == 0:
            loads[1].wait()
        mid[rows, :] = (group.astype(F32) + dot(mixed[...], w_o[...])).astype(BF16)

    def read_part(g):
        if g == 0:
            loads[2].wait()
            query = dot(rms_norm(lat_in[...], g_lat[...]), w_qr[...]).astype(BF16)
            rq[...] = query * jnp.asarray(SCALE, BF16)
            loads[3].wait()
        rows = pl.ds(g * G, G)
        lrows = pl.ds(g * NLAT, NLAT)
        kvr[...] = dot(rms_norm(mid[rows, :], g_read[...]), w_kvr[...]).astype(BF16)
        quad = 4 * HEAD
        for at in range(0, lat_width, quad):
            out = softmax_mix(
                spread_heads(rq[lrows, at : at + quad], 4),
                kvr[:, at : at + quad],
                kvr[:, lat_width + at : lat_width + at + quad],
            )
            lmid[lrows, at : at + quad] = (
                lat_in[lrows, at : at + quad].astype(F32) + fold_heads(out, 4)
            ).astype(BF16)
        gath[g, core, me] = rms_norm(lmid[lrows, :], g_glob[...])
        z_start(g)

    pending = []

    def advance():
        for i, (g, stage) in enumerate(pending):
            if stage < 3:
                (stage_one, stage_two, stage_three)[stage](g)
                pending[i] = (g, stage + 1)

    for g in range(groups):
        self_part(g)
        advance()
        read_part(g)
        advance()
        if g == groups - 2:
            wo_first[1].wait_recv()
            wo_relay.start()
        pending.append((g, 0))

    block_rows = 4 * nz * NLAT
    tile = min(block_rows, G)
    blocks = tile // NLAT

    def project(g, c):
        def one(i, carry):
            rows = gath[g, c, pl.ds(i * blocks, blocks)].reshape(tile, lat_width)
            at = pl.multiple_of((g * 2 + c) * block_rows + i * tile, tile)
            kv[0, pl.ds(at, tile), :] = dot(rows, w_glob[1]).astype(BF16)
            kv[1, pl.ds(at, tile), :] = dot(rows, w_glob[2]).astype(BF16)
            return carry

        lax.fori_loop(0, block_rows // tile, one, 0)

    loads[5].wait()
    for g in range(groups):
        rows = pl.ds(g * G, G)
        query = dot(rms_norm(mid[rows, :], g_write[...]), w_qw[...]).astype(BF16)
        tok_out[rows, :] = query * jnp.asarray(SCALE, BF16)
    advance()
    loads[4].wait()
    for g in range(groups):
        while pending[g][1] < 3:
            advance()
        for c in range(3):
            shares[g][c].wait_recv()
        project(g, 0)
        project(g, 1)

    own = []
    for l in range(lat_count):
        ly, lc = l // 2, l % 2
        index = ((x * 2 + ly) if lc == 0 else (ly * 2 + x)) * nz + z
        for g in range(groups):
            own.append(gath[g, lc, index])
    query = dot(jnp.concatenate(own, axis=0), w_glob[0]).astype(BF16) * jnp.asarray(SCALE, BF16)
    heads = query.shape[1] // HEAD
    qq[...] = spread_heads(query, heads)
    part = lat_rows * lat_count if kv.shape[1] * lat_rows * lat_count <= 2**20 else lat_rows

    def attend(i, carry):
        rows = pl.ds(pl.multiple_of(i * part, part), part)
        qq[rows, :] = softmax_mix(qq[rows, :], kv[0], kv[1]).astype(BF16)
        return carry

    lax.fori_loop(0, qq.shape[0] // part, attend, 0)
    result = fold_heads(qq[...], heads)
    for l in range(lat_count):
        msend[l] = result[l * lat_rows : (l + 1) * lat_rows]
    mix_copies = []
    for i, peer in enumerate((partner, lat_y, diag)):
        mix_copies.append(remote(msend.at[peer], mrecv.at[lat], m_send.at[i], m_recv.at[i], (dp, peer)))
        mix_copies[-1].start()
    mrecv[lat] = msend[lat]
    loads[7].wait()
    loads[6].wait()
    wo_first[0].wait_recv()
    wo_relay.wait_recv()
    for copy in mix_copies:
        copy.wait_recv()
    total = dot(mrecv[0], w_og[0])
    for l in range(1, lat_count):
        total = total + dot(mrecv[l], w_og[l])
    final = (lmid[...].astype(F32) + total).astype(BF16)
    lat_out[...] = final
    lfin[...] = dot(rms_norm(final, g_wlat[...]), w_kvw[...]).astype(BF16)

    heads = width // HEAD
    for g in range(groups):
        rows = pl.ds(g * G, G)
        lrows = pl.ds(g * NLAT, NLAT)
        keys = spread_heads(lfin[lrows, :width], heads)
        values = spread_heads(lfin[lrows, width:], heads)
        scores = dot_nt(keys, tok_out[rows, :]).reshape(heads, NLAT, G)
        peak = jnp.max(scores, axis=1, keepdims=True)
        weights = jnp.exp(scores - peak)
        weights = weights * (1.0 / jnp.sum(weights, axis=1, keepdims=True))
        written = dot_tn(weights.reshape(heads * NLAT, G).astype(BF16), values)
        tok_out[rows, :] = (mid[rows, :].astype(F32) + written).astype(BF16)

    for copy in wo_first + [wo_relay] + mix_copies:
        copy.wait_send()
    for g in range(groups):
        z_wait(g, z_send)
        to_first[g].wait_send()
        to_second[g].wait_send()
        for copy in shares[g]:
            copy.wait_send()


def local(
    tokens, latents, gain_self, w_qkv_tok, w_o_tok, gain_read, w_kv_read, gain_lat, w_q_read,
    gain_glob, w_qkv_glob, w_o_glob, gain_write, w_q_write, gain_wlat, w_kv_write,
):
    dp_count = lax.axis_size("dp")
    lat_count = lax.axis_size("lat")
    rows, width = tokens.shape
    lat_rows, lat_width = latents.shape
    groups = rows // G
    here = w_qkv_glob.shape[2]
    nz = dp_count // 2
    all_rows = lat_rows * dp_count * lat_count
    vmem = pl.BlockSpec(memory_space=pltpu.VMEM)
    hbm = pl.BlockSpec(memory_space=pl.ANY)
    dma = pltpu.SemaphoreType.DMA
    return pl.pallas_call(
        functools.partial(kernel, dp_count, lat_count),
        out_shape=(
            jax.ShapeDtypeStruct(tokens.shape, BF16),
            jax.ShapeDtypeStruct(latents.shape, BF16),
        ),
        in_specs=[vmem, vmem, vmem, hbm, hbm, vmem, hbm, vmem, hbm, vmem, hbm, hbm, vmem, hbm, vmem, hbm],
        out_specs=(vmem, vmem),
        scratch_shapes=[
            pltpu.VMEM(w_qkv_tok.shape, BF16),
            pltpu.VMEM(w_o_tok.shape, BF16),
            pltpu.VMEM(w_kv_read.shape, BF16),
            pltpu.VMEM(w_q_read.shape, BF16),
            pltpu.VMEM(w_qkv_glob.shape, BF16),
            pltpu.VMEM((lat_count,) + w_o_glob.shape, BF16),
            pltpu.VMEM(w_q_write.shape, BF16),
            pltpu.VMEM(w_kv_write.shape, BF16),
            pltpu.VMEM(tokens.shape, BF16),
            pltpu.VMEM(latents.shape, BF16),
            pltpu.VMEM(latents.shape, BF16),
            pltpu.VMEM((G, w_qkv_tok.shape[1]), BF16),
            pltpu.VMEM((G, width), BF16),
            pltpu.VMEM((G, w_kv_read.shape[1]), BF16),
            pltpu.VMEM((groups, 2, 4 * nz, NLAT, lat_width), BF16),
            pltpu.VMEM((2, all_rows, here), BF16),
            pltpu.VMEM((lat_rows * lat_count * (here // HEAD), here), BF16),
            pltpu.VMEM((lat_count, lat_rows, here), BF16),
            pltpu.VMEM((lat_count, lat_rows, here), BF16),
            pltpu.VMEM((lat_rows, w_kv_write.shape[1]), BF16),
            dma((8,)),
            dma((groups,)),
            dma((groups,)),
            dma((groups, 2)),
            dma((groups, 2)),
            dma((groups, 3)),
            dma((groups, 3)),
            dma((3,)),
            dma((3,)),
            dma((3,)),
            dma((3,)),
        ],
        compiler_params=pltpu.CompilerParams(
            collective_id=0, has_side_effects=True, vmem_limit_bytes=67043328
        ),
    )(
        tokens, latents, gain_self[None], w_qkv_tok, w_o_tok, gain_read[None], w_kv_read,
        gain_lat[None], w_q_read, gain_glob[None], w_qkv_glob, w_o_glob, gain_write[None],
        w_q_write, gain_wlat[None], w_kv_write,
    )


def solution(mesh):
    rows = P(("dp", "lat"), None)
    whole = P()
    placed = (
        rows, rows, whole, whole, whole, whole, whole, whole, whole, whole,
        P(None, None, "lat"), P("lat", None), whole, whole, whole, whole,
    )
    return jax.shard_map(
        local, mesh=mesh, in_specs=placed, out_specs=(rows, rows), check_vma=False
    )
```

time: 141 us -> 65.8 us (0.47)
  Pallas kernels: 0 us -> 61.3 us
  matrix products: 33 us -> 0 us
  waiting for transfers between devices: 25.7 us -> 0 us
  blocking collectives: 18.1 us -> 0 us
  local copies, waits for them, and re-layouts: 21.4 us -> 3.6 us
  between operations: 14.5 us -> 0.65 us
  other arithmetic: 13.8 us -> 0 us
  starting transfers between devices: 12.9 us -> 0 us
    pallas_call x0 -> x1, Pallas kernels: none -> 61.3 us  [local(): pl.pallas_call(functools.partial(kernel, dp_count, lat_count), out_shape=...]
    dot_general x15 -> x0, matrix products: 28.8 us -> none  [the longest x4 5.68 us: attend(): jnp.einsum('hqk,khe->hqe', weights.astype(jnp.bfloat16), values, preferre...]
    reduce_scatter x1 -> x0, waiting for transfers between devices: 14.4 us -> none  [local(): lax.psum_scatter(jnp.dot(mixed, w_o_glob, preferred_element_type=jnp.floa...]
    all_to_all x3 -> x0, starting transfers between devices: 12.9 us -> none  [the longest x1 5.82 us: local(): lax.all_to_all(query_send, 'dp', split_axis=0, concat_axis=0, tiled=True)]
    all_to_all x3 -> x0, waiting for transfers between devices: 11.2 us -> none  [the longest x1 5.71 us: local(): lax.all_to_all(fan_out(head_major(2)), 'dp', split_axis=0, concat_axis=0,...]
    convert_element_type x8 -> x0, local copies, waits for them, and re-layouts: 11 us -> none  [the longest x1 4.73 us: front(): key_vals = key_vals.astype(jnp.bfloat16).reshape(rows, 2, -1, HEAD)]
    all_to_all x1 -> x0, blocking collectives: 10.2 us -> none  [local(): lax.all_to_all(mixed_rows.reshape(dp_count, item_count, HEAD), 'dp', spli...]
    all_gather x1 -> x0, blocking collectives: 7.97 us -> none  [local(): block = lax.all_gather(normed, 'lat', axis=0, tiled=True)]
  transfers between devices with their start and end apart: 4 -> 0, of which waited for: 4 -> 0; matrix products, arithmetic and copies ran while one was open for 11% -> 0% of each run, Pallas kernels for 0% -> 0%
where the time goes in v1:
time: 65.8 us; the launch traced here: 65.6 us
  Pallas kernels  61.3 us (93%)
  local copies, waits for them, and re-layouts  3.6 us (5%)
    pallas_call x1, Pallas kernels, local(): pl.pallas_call(functools.partial(kernel, dp_count, lat_count), out_shape=...  61.3 us
    unnamed x2, local copies, waits for them, and re-layouts  3.6 us

profile of v1, /device:TPU:0, one launch (start us, length us, event | category | flops | bytes accessed | tf_op | source)
XLA Modules:
  0.0 65.6 jit_solution(9582549766734387597)
XLA Ops:
  0.6 61.3 %shard_map.167 = (bf16[768,512]{1,0:T(8,128)(2,1)}, bf16[48,1024]{1,0:T(8,128)(2,1)}) custom-call(bf16[768,512]{1,0:T(8,128)(2,1)} %tok.1, bf16[48,1024]{1,0:T(8,128)(2,1)} %lat_in.1, f32[1,512]{1,0:T(1,128)} %bitcast.9, bf16[512,1536]{1,0:T(8,128)(2,1)} %w_qkv_h.1, bf16[512,512]{1,0:T(8,128)(2,1)} %w_o_h.1, f32[1,512]{1,0:T(1,128)} %bitcast.10, ...), custom_call_target="tpu_custom_call" | custom-call | tf_op jit(solution)/shard_map/pallas_call | solution.py:381
  62.0 2.1 %copy.20 = bf16[768,512]{1,0:T(8,128)(2,1)} copy(bf16[768,512]{1,0:T(8,128)(2,1)} %get-tuple-element.4) | data formatting | bytes 1572864
  64.1 1.5 %copy.21 = bf16[48,1024]{1,0:T(8,128)(2,1)} copy(bf16[48,1024]{1,0:T(8,128)(2,1)} %get-tuple-element.5) | data formatting | bytes 196608

commit v2 on v1

--- a/solution.py
+++ b/solution.py
@@ -12,6 +12,7 @@
 NLAT = 16
 SCALE = HEAD ** (-0.5)
 MESH = pl.DeviceIdType.MESH
+PARTS = 4
 F32 = jnp.float32
 BF16 = jnp.bfloat16
 
@@ -98,11 +99,16 @@
     msend,
     mrecv,
     lfin,
+    top,
+    norm,
+    acc,
     load_sem,
     z_send,
     z_recv,
-    p_send,
-    p_recv,
+    f_send,
+    f_recv,
+    s_send,
+    s_recv,
     c_send,
     c_recv,
     wo_send,
@@ -130,6 +136,8 @@
     base = (b * 2 + a) * nz
     other = (b * 2 + 1 - a) * nz
     me = base + z
+    far = (1 - 2 * b) * 2 * nz
+    run = nz // PARTS
 
     loads = []
     for i, (src, dst) in enumerate(
@@ -172,48 +180,77 @@
     def along(ref, send_sem, recv_sem, peer):
         return remote(ref, ref, send_sem, recv_sem, peer)
 
-    to_first = [along(piece(g, base, nz), p_send.at[g, 0], p_recv.at[g, 0], first) for g in range(groups)]
-    to_second = [
-        along(piece(g, b * 2 * nz, 2 * nz), p_send.at[g, 1], p_recv.at[g, 1], second)
-        for g in range(groups)
-    ]
-    shares = [
-        [
-            along(piece(g, start, count), c_send.at[g, i], c_recv.at[g, i], (dp, partner))
-            for i, (start, count) in enumerate(
-                ((base, nz), (other, nz), ((1 - b) * 2 * nz, 2 * nz))
-            )
-        ]
-        for g in range(groups)
-    ]
+    def on_first(g, p):
+        return along(
+            piece(g, base + p * run, run), f_send.at[g, p], f_recv.at[g, p], first
+        )
+
+    def on_second(g, half, p):
+        start = base + (other - base) * half + p * run
+        k = half * PARTS + p
+        return along(piece(g, start, run), s_send.at[g, k], s_recv.at[g, k], second)
+
+    def share(g, line, p):
+        start = (base, other, base + far, other + far)[line] + p * run
+        k = line * PARTS + p
+        return along(
+            piece(g, start, run), c_send.at[g, k], c_recv.at[g, k], (dp, partner)
+        )
+
+    def z_copy(g, offset):
+        return remote(
+            gath.at[g, core, me], gath.at[g, core, me], z_send.at[g, (z + offset) % nz],
+            z_recv.at[g, z], ((z + offset) % nz * 2 + x, lat),
+        )
+
+    def each(low, high, body):
+        def one(i, carry):
+            body(i)
+            return carry
+
+        lax.fori_loop(low, high, one, 0)
 
     def z_start(g):
-        def one(offset, carry):
-            remote(
-                gath.at[g, core, me], gath.at[g, core, me], z_send.at[g], z_recv.at[g],
-                ((z + offset) % nz * 2 + x, lat),
-            ).start()
-            return carry
-
-        lax.fori_loop(1, nz, one, 0)
-
-    def z_wait(g, sem):
-        ref = piece(g, base, nz - 1)
-        pltpu.make_async_copy(ref, ref, sem.at[g]).wait()
-
-    def stage_one(g):
-        z_wait(g, z_recv)
-        to_first[g].start()
-        shares[g][0].start()
+        each(1, nz, lambda offset: z_copy(g, offset).start())
+
+    def z_arrived(g, block):
+        ref = piece(g, base + block, 1)
+
+        @pl.when(block != z)
+        def _():
+            pltpu.make_async_copy(ref, ref, z_recv.at[g, block]).wait()
+
+    def stage_one(g, low, high):
+        def body(o):
+            p = (z // run + o) % PARTS
+            each(0, run, lambda i: z_arrived(g, p * run + i))
+            on_first(g, p).start()
+            on_second(g, 0, p).start()
+            share(g, 0, p).start()
+
+        each(low, high, body)
 
     def stage_two(g):
-        to_first[g].wait_recv()
-        to_second[g].start()
-        shares[g][1].start()
+        def body(o):
+            p = (z // run + o) % PARTS
+            on_first(g, p).wait_recv()
+            on_second(g, 1, p).start()
+            share(g, 1, p).start()
+
+        each(0, PARTS, body)
+
+    def second_arrived(g, half, o):
+        p = (z // run + o) % PARTS
+        on_second(g, half, p).wait_recv()
+        share(g, 2 + half, p).start()
 
     def stage_three(g):
-        to_second[g].wait_recv()
-        shares[g][2].start()
+        for half in range(2):
+            each(0, PARTS, lambda o: second_arrived(g, half, o))
+
+    def gathered(g):
+        for line in range(4):
+            each(0, PARTS, lambda p: share(g, line, p).wait_recv())
 
     def self_part(g):
         rows = pl.ds(g * G, G)
@@ -254,24 +291,17 @@
             ).astype(BF16)
         gath[g, core, me] = rms_norm(lmid[lrows, :], g_glob[...])
         z_start(g)
-
-    pending = []
-
-    def advance():
-        for i, (g, stage) in enumerate(pending):
-            if stage < 3:
-                (stage_one, stage_two, stage_three)[stage](g)
-                pending[i] = (g, stage + 1)
-
+        stage_one(g, 0, 1)
+
+    last = groups - 1
     for g in range(groups):
         self_part(g)
-        advance()
+        if g >= 2:
+            stage_one(g - 2, 1, PARTS)
+            if g == 2:
+                wo_first[1].wait_recv()
+                wo_relay.start()
         read_part(g)
-        advance()
-        if g == groups - 2:
-            wo_first[1].wait_recv()
-            wo_relay.start()
-        pending.append((g, 0))
 
     block_rows = 4 * nz * NLAT
     tile = min(block_rows, G)
@@ -287,20 +317,41 @@
 
         lax.fori_loop(0, block_rows // tile, one, 0)
 
+    for g in range(last - 1):
+        stage_two(g)
     loads[5].wait()
     for g in range(groups):
         rows = pl.ds(g * G, G)
         query = dot(rms_norm(mid[rows, :], g_write[...]), w_qw[...]).astype(BF16)
         tok_out[rows, :] = query * jnp.asarray(SCALE, BF16)
-    advance()
+    stage_one(last - 1, 1, PARTS)
     loads[4].wait()
-    for g in range(groups):
-        while pending[g][1] < 3:
-            advance()
-        for c in range(3):
-            shares[g][c].wait_recv()
+    for g in range(last - 1):
+        stage_three(g)
+    stage_two(last - 1)
+    for g in range(last - 1):
+        gathered(g)
         project(g, 0)
         project(g, 1)
+    stage_one(last, 1, PARTS)
+    stage_two(last)
+    stage_three(last - 1)
+    gathered(last - 1)
+    project(last - 1, 0)
+    project(last - 1, 1)
+    own_p = z // run
+
+    @pl.when(core == 1)
+    def _():
+        on_second(last, 0, own_p).wait_recv()
+        share(last, 2, own_p).start()
+        for line in range(2):
+            share(last, line, own_p).wait_recv()
+
+    @pl.when(core == 0)
+    def _():
+        for line in (0, 2):
+            share(last, line, own_p).wait_recv()
 
     own = []
     for l in range(lat_count):
@@ -311,14 +362,53 @@
     query = dot(jnp.concatenate(own, axis=0), w_glob[0]).astype(BF16) * jnp.asarray(SCALE, BF16)
     heads = query.shape[1] // HEAD
     qq[...] = spread_heads(query, heads)
-    part = lat_rows * lat_count if kv.shape[1] * lat_rows * lat_count <= 2**20 else lat_rows
-
-    def attend(i, carry):
+    early = last * 2 * block_rows
+    full = lat_rows * lat_count
+    part = full if early * full <= 2**20 else lat_rows
+
+    def attend_early(i, carry):
         rows = pl.ds(pl.multiple_of(i * part, part), part)
-        qq[rows, :] = softmax_mix(qq[rows, :], kv[0], kv[1]).astype(BF16)
+        scores = dot_nt(qq[rows, :], kv[0, :early, :])
+        peak = jnp.max(scores, axis=-1, keepdims=True)
+        weights = jnp.exp(scores - peak)
+        top[rows, :] = peak
+        norm[rows, :] = jnp.sum(weights, axis=-1, keepdims=True)
+        acc[rows, :] = dot(weights.astype(BF16), kv[1, :early, :])
         return carry
 
-    lax.fori_loop(0, qq.shape[0] // part, attend, 0)
+    def attend_late(i, carry):
+        rows = pl.ds(pl.multiple_of(i * part, part), part)
+        scores = dot_nt(qq[rows, :], kv[0, early:, :])
+        peak = jnp.maximum(top[rows, :], jnp.max(scores, axis=-1, keepdims=True))
+        weights = jnp.exp(scores - peak)
+        keep = jnp.exp(top[rows, :] - peak)
+        total = norm[rows, :] * keep + jnp.sum(weights, axis=-1, keepdims=True)
+        both = acc[rows, :] * keep + dot(weights.astype(BF16), kv[1, early:, :])
+        qq[rows, :] = (both * (1.0 / total)).astype(BF16)
+        return carry
+
+    lax.fori_loop(0, qq.shape[0] // part, attend_early, 0)
+
+    @pl.when(core == 1)
+    def _():
+        each(1, PARTS, lambda o: second_arrived(last, 0, o))
+        each(0, PARTS, lambda o: second_arrived(last, 1, o))
+        for line in range(2):
+            each(1, PARTS, lambda o: share(last, line, (own_p + o) % PARTS).wait_recv())
+        for line in range(2, 4):
+            each(0, PARTS, lambda p: share(last, line, p).wait_recv())
+
+    @pl.when(core == 0)
+    def _():
+        stage_three(last)
+        for line in (0, 2):
+            each(1, PARTS, lambda o: share(last, line, (own_p + o) % PARTS).wait_recv())
+        for line in (1, 3):
+            each(0, PARTS, lambda p: share(last, line, p).wait_recv())
+
+    project(last, 0)
+    project(last, 1)
+    lax.fori_loop(0, qq.shape[0] // part, attend_late, 0)
     result = fold_heads(qq[...], heads)
     for l in range(lat_count):
         msend[l] = result[l * lat_rows : (l + 1) * lat_rows]
@@ -356,11 +446,16 @@
     for copy in wo_first + [wo_relay] + mix_copies:
         copy.wait_send()
     for g in range(groups):
-        z_wait(g, z_send)
-        to_first[g].wait_send()
-        to_second[g].wait_send()
-        for copy in shares[g]:
-            copy.wait_send()
+        each(1, nz, lambda offset: z_copy(g, offset).wait_send())
+
+        def sent(p):
+            on_first(g, p).wait_send()
+            for half in range(2):
+                on_second(g, half, p).wait_send()
+            for line in range(4):
+                share(g, line, p).wait_send()
+
+        each(0, PARTS, sent)
 
 
 def local(
@@ -407,13 +502,18 @@
             pltpu.VMEM((lat_count, lat_rows, here), BF16),
             pltpu.VMEM((lat_count, lat_rows, here), BF16),
             pltpu.VMEM((lat_rows, w_kv_write.shape[1]), BF16),
+            pltpu.VMEM((lat_rows * lat_count * (here // HEAD), 1), F32),
+            pltpu.VMEM((lat_rows * lat_count * (here // HEAD), 1), F32),
+            pltpu.VMEM((lat_rows * lat_count * (here // HEAD), here), F32),
             dma((8,)),
-            dma((groups,)),
-            dma((groups,)),
-            dma((groups, 2)),
-            dma((groups, 2)),
-            dma((groups, 3)),
-            dma((groups, 3)),
+            dma((groups, nz)),
+            dma((groups, nz)),
+            dma((groups, PARTS)),
+            dma((groups, PARTS)),
+            dma((groups, 2 * PARTS)),
+            dma((groups, 2 * PARTS)),
+            dma((groups, 4 * PARTS)),
+            dma((groups, 4 * PARTS)),
             dma((3,)),
             dma((3,)),
             dma((3,)),

time: 65.8 us -> 57.2 us (0.87)
  Pallas kernels: 61.3 us -> 52.8 us
    pallas_call x1, Pallas kernels: 61.3 us -> 52.8 us  [local(): pl.pallas_call(functools.partial(kernel, dp_count, lat_count), out_shape=...]
where the time goes in v2:
time: 57.2 us; the launch traced here: 57 us
  Pallas kernels  52.8 us (92%)
  local copies, waits for them, and re-layouts  3.6 us (6%)
  between operations  0.65 us (1%)
    pallas_call x1, Pallas kernels, local(): pl.pallas_call(functools.partial(kernel, dp_count, lat_count), out_shape=...  52.8 us
    unnamed x2, local copies, waits for them, and re-layouts  3.6 us

profile of v2, /device:TPU:0, one launch (start us, length us, event | category | flops | bytes accessed | tf_op | source)
XLA Modules:
  0.0 57.0 jit_solution(3917254390913878596)
XLA Ops:
  0.6 52.8 %shard_map.167 = (bf16[768,512]{1,0:T(8,128)(2,1)}, bf16[48,1024]{1,0:T(8,128)(2,1)}) custom-call(bf16[768,512]{1,0:T(8,128)(2,1)} %tok.1, bf16[48,1024]{1,0:T(8,128)(2,1)} %lat_in.1, f32[1,512]{1,0:T(1,128)} %bitcast.9, bf16[512,1536]{1,0:T(8,128)(2,1)} %w_qkv_h.1, bf16[512,512]{1,0:T(8,128)(2,1)} %w_o_h.1, f32[1,512]{1,0:T(1,128)} %bitcast.10, ...), custom_call_target="tpu_custom_call" | custom-call | tf_op jit(solution)/shard_map/pallas_call | solution.py:476
  53.4 2.1 %copy.20 = bf16[768,512]{1,0:T(8,128)(2,1)} copy(bf16[768,512]{1,0:T(8,128)(2,1)} %get-tuple-element.4) | data formatting | bytes 1572864
  55.5 1.5 %copy.21 = bf16[48,1024]{1,0:T(8,128)(2,1)} copy(bf16[48,1024]{1,0:T(8,128)(2,1)} %get-tuple-element.5) | data formatting | bytes 196608

commit v3 on v2

--- a/solution.py
+++ b/solution.py
@@ -79,6 +79,8 @@
     w_kvw_h,
     tok_out,
     lat_out,
+    mid,
+    lfin,
     w_qkv,
     w_o,
     w_kvr,
@@ -87,7 +89,6 @@
     w_og,
     w_qw,
     w_kvw,
-    mid,
     lmid,
     rq,
     packed,
@@ -98,7 +99,6 @@
     qq,
     msend,
     mrecv,
-    lfin,
     top,
     norm,
     acc,
@@ -430,19 +430,6 @@
     lat_out[...] = final
     lfin[...] = dot(rms_norm(final, g_wlat[...]), w_kvw[...]).astype(BF16)
 
-    heads = width // HEAD
-    for g in range(groups):
-        rows = pl.ds(g * G, G)
-        lrows = pl.ds(g * NLAT, NLAT)
-        keys = spread_heads(lfin[lrows, :width], heads)
-        values = spread_heads(lfin[lrows, width:], heads)
-        scores = dot_nt(keys, tok_out[rows, :]).reshape(heads, NLAT, G)
-        peak = jnp.max(scores, axis=1, keepdims=True)
-        weights = jnp.exp(scores - peak)
-        weights = weights * (1.0 / jnp.sum(weights, axis=1, keepdims=True))
-        written = dot_tn(weights.reshape(heads * NLAT, G).astype(BF16), values)
-        tok_out[rows, :] = (mid[rows, :].astype(F32) + written).astype(BF16)
-
     for copy in wo_first + [wo_relay] + mix_copies:
         copy.wait_send()
     for g in range(groups):
@@ -456,6 +443,20 @@
                 share(g, line, p).wait_send()
 
         each(0, PARTS, sent)
+
+
+def back(query, final, mid, key_vals, tok_out, lat_out):
+    width = query.shape[1]
+    heads = width // HEAD
+    keys = spread_heads(key_vals[:, :width], heads)
+    values = spread_heads(key_vals[:, width:], heads)
+    scores = dot_nt(keys, query[...]).reshape(heads, NLAT, G)
+    peak = jnp.max(scores, axis=1, keepdims=True)
+    weights = jnp.exp(scores - peak)
+    weights = weights * (1.0 / jnp.sum(weights, axis=1, keepdims=True))
+    written = dot_tn(weights.reshape(heads * NLAT, G).astype(BF16), values)
+    tok_out[...] = (mid[...].astype(F32) + written).astype(BF16)
+    lat_out[...] = final[...]
 
 
 def local(
@@ -473,14 +474,16 @@
     vmem = pl.BlockSpec(memory_space=pltpu.VMEM)
     hbm = pl.BlockSpec(memory_space=pl.ANY)
     dma = pltpu.SemaphoreType.DMA
-    return pl.pallas_call(
+    query, final, mid, key_vals = pl.pallas_call(
         functools.partial(kernel, dp_count, lat_count),
         out_shape=(
             jax.ShapeDtypeStruct(tokens.shape, BF16),
             jax.ShapeDtypeStruct(latents.shape, BF16),
+            jax.ShapeDtypeStruct(tokens.shape, BF16),
+            jax.ShapeDtypeStruct((lat_rows, w_kv_write.shape[1]), BF16),
         ),
         in_specs=[vmem, vmem, vmem, hbm, hbm, vmem, hbm, vmem, hbm, vmem, hbm, hbm, vmem, hbm, vmem, hbm],
-        out_specs=(vmem, vmem),
+        out_specs=(vmem,) * 4,
         scratch_shapes=[
             pltpu.VMEM(w_qkv_tok.shape, BF16),
             pltpu.VMEM(w_o_tok.shape, BF16),
@@ -490,7 +493,6 @@
             pltpu.VMEM((lat_count,) + w_o_glob.shape, BF16),
             pltpu.VMEM(w_q_write.shape, BF16),
             pltpu.VMEM(w_kv_write.shape, BF16),
-            pltpu.VMEM(tokens.shape, BF16),
             pltpu.VMEM(latents.shape, BF16),
             pltpu.VMEM(latents.shape, BF16),
             pltpu.VMEM((G, w_qkv_tok.shape[1]), BF16),
@@ -501,7 +503,6 @@
             pltpu.VMEM((lat_rows * lat_count * (here // HEAD), here), BF16),
             pltpu.VMEM((lat_count, lat_rows, here), BF16),
             pltpu.VMEM((lat_count, lat_rows, here), BF16),
-            pltpu.VMEM((lat_rows, w_kv_write.shape[1]), BF16),
             pltpu.VMEM((lat_rows * lat_count * (here // HEAD), 1), F32),
             pltpu.VMEM((lat_rows * lat_count * (here // HEAD), 1), F32),
             pltpu.VMEM((lat_rows * lat_count * (here // HEAD), here), F32),
@@ -527,6 +528,23 @@
         gain_lat[None], w_q_read, gain_glob[None], w_qkv_glob, w_o_glob, gain_write[None],
         w_q_write, gain_wlat[None], w_kv_write,
     )
+    per_group = pl.BlockSpec((G, width), lambda g: (g, 0))
+    per_lat = pl.BlockSpec((NLAT, lat_width), lambda g: (g, 0))
+    return pl.pallas_call(
+        back,
+        grid=(groups,),
+        out_shape=(
+            jax.ShapeDtypeStruct(tokens.shape, BF16),
+            jax.ShapeDtypeStruct(latents.shape, BF16),
+        ),
+        in_specs=[
+            per_group,
+            per_lat,
+            per_group,
+            pl.BlockSpec((NLAT, key_vals.shape[1]), lambda g: (g, 0)),
+        ],
+        out_specs=(per_group, per_lat),
+    )(query, final, mid, key_vals)
 
 
 def solution(mesh):

time: 57.2 us -> 56.9 us (level)
  local copies, waits for them, and re-layouts: 3.6 us -> 0 us
  Pallas kernels: 52.8 us -> 56 us
    pallas_call x0 -> x1, Pallas kernels: none -> 4.15 us  [local(): pl.pallas_call(back, grid=(groups,), out_shape=(jax.ShapeDtypeStruct(toke...]
    unnamed x2 -> x0, local copies, waits for them, and re-layouts: 3.6 us -> none
    pallas_call x1, Pallas kernels: 52.8 us -> 51.9 us  [local(): pl.pallas_call(functools.partial(kernel, dp_count, lat_count), out_shape=...]
where the time goes in v3:
time: 56.9 us; the launch traced here: 56.7 us
  Pallas kernels  56 us (98%)
  between operations  0.64 us (1%)
    pallas_call x1, Pallas kernels, local(): pl.pallas_call(functools.partial(kernel, dp_count, lat_count), out_shape=...  51.9 us
    pallas_call x1, Pallas kernels, local(): pl.pallas_call(back, grid=(groups,), out_shape=(jax.ShapeDtypeStruct(toke...  4.15 us

profile of v3, /device:TPU:0, one launch (start us, length us, event | category | flops | bytes accessed | tf_op | source)
XLA Modules:
  0.0 56.7 jit_solution(8345326458441282973)
XLA Ops:
  0.6 51.9 %shard_map.167 = (bf16[768,512]{1,0:T(8,128)(2,1)}, bf16[48,1024]{1,0:T(8,128)(2,1)}, bf16[768,512]{1,0:T(8,128)(2,1)}, bf16[48,1024]{1,0:T(8,128)(2,1)}) custom-call(bf16[768,512]{1,0:T(8,128)(2,1)} %tok.1, bf16[48,1024]{1,0:T(8,128)(2,1)} %lat_in.1, f32[1,512]{1,0:T(1,128)} %bitcast.9, bf16[512,1536]{1,0:T(8,128)(2,1)} %w_qkv_h.1, bf16[512,512]{1,0:T(8,128)(2,1)} %w_o_h.1, ...), custom_call_target="tpu_custom_call" | custom-call | tf_op jit(solution)/shard_map/pallas_call | solution.py:477
  52.5 4.2 %shard_map.168 = (bf16[768,512]{1,0:T(8,128)(2,1)}, bf16[48,1024]{1,0:T(8,128)(2,1)}) custom-call(bf16[768,512]{1,0:T(8,128)(2,1)} %get-tuple-element.6.query, bf16[48,1024]{1,0:T(8,128)(2,1)} %get-tuple-element.7.final, bf16[768,512]{1,0:T(8,128)(2,1)} %get-tuple-element.8.mid, bf16[48,1024]{1,0:T(8,128)(2,1)} %get-tuple-element.9.key_vals), custom_call_target="tpu_custom_call" | custom-call | tf_op jit(solution)/shard_map/pallas_call | solution.py:533
